TPU v7x, 32 devices: a whole 2x2x4 slice. The times are simulated.
32 devices in a mesh: row: 4 (over x, core), col: 8 (over z, y).
Axes of the slice: x: 2, y: 2, z: 4, core: 2. Of those that a mesh axis runs over, the one named last changes fastest.
Arguments:
- vectors: float32 [16, 4096], P(None, ('row', 'col')), may hold values from -12 to 12, as said below
- diag_energy: float32 [4096], P(('row', 'col')), may hold values from 0.5 to 4
- blocks: float32 [4, 192, 128, 128], P('row', 'col'), may hold values from -0.078125 to 0.078125
- block_row: int32 [4, 192], P('row', 'col'), may hold values from 0 to 7
- block_col: int32 [4, 192], P('row', 'col'), may hold values from 0 to 3
Outputs:
- image: float32 [16, 4096], P(None, ('row', 'col'))
- resid: float32 [16, 4096], P(None, ('row', 'col'))
Inputs may be any that keep to these rules, and one draw needn't show every extreme that they name: `vectors`: each row of X holds independent entries; the Gram matrix X X^T is positive definite.
All inputs are finite; a program needn't handle non-finite values.
Results may differ from a plain program's by a relative error of at most 0.0003.
Values sent between devices are 32-bit elements; how exact they have to be, the bound alone decides.
A program may use at most 64 MiB of HBM per device.

v0:
```python
import jax
import jax.numpy as jnp
from jax import lax
from jax.sharding import PartitionSpec as P

BLK = 128


def solve_metric(metric, gram):
    highest = lax.Precision.HIGHEST
    order = metric.shape[0]
    index = jnp.arange(order)
    factor = jnp.zeros_like(metric)
    for column in range(order):
        onehot = (index == column).astype(jnp.float32)
        rest = metric[:, column] - jnp.dot(factor, factor[column, :], precision=highest)
        pivot = jnp.sqrt(rest[column])
        values = jnp.where(index >= column, rest / pivot, 0.0)
        factor = factor + values[:, None] * onehot[None, :]
    inner = jnp.zeros_like(gram)
    for line in range(order):
        onehot = (index == line).astype(jnp.float32)
        value = (gram[line, :] - jnp.dot(factor[line, :], inner, precision=highest)) / factor[
            line, line
        ]
        inner = inner + onehot[:, None] * value[None, :]
    solved = jnp.zeros_like(gram)
    for line in range(order - 1, -1, -1):
        onehot = (index == line).astype(jnp.float32)
        value = (inner[line, :] - jnp.dot(factor[:, line], solved, precision=highest)) / factor[
            line, line
        ]
        solved = solved + onehot[:, None] * value[None, :]
    return solved


def per_device(vectors, diag_energy, blocks, block_row, block_col):
    highest = lax.Precision.HIGHEST
    count = vectors.shape[0]
    tiles = blocks[0]
    rows_here = block_row[0]
    cols_here = block_col[0]
    col_whole = lax.all_gather(vectors, "row", axis=1, tiled=True)
    row_whole = lax.all_gather(vectors, "col", axis=1, tiled=True)
    row_blocks = row_whole.shape[1] // BLK
    col_blocks = col_whole.shape[1] // BLK
    col_split = col_whole.reshape(count, col_blocks, BLK)
    row_split = row_whole.reshape(count, row_blocks, BLK)
    picked = col_split[:, cols_here]
    terms = jnp.einsum("bij,kbj->kbi", tiles, picked, precision=highest)
    onehot = (rows_here[:, None] == jnp.arange(row_blocks)[None, :]).astype(jnp.float32)
    part_one = jnp.einsum("kbi,br->kri", terms, onehot, precision=highest).reshape(
        count, row_blocks * BLK
    )
    picked_two = row_split[:, rows_here]
    terms_two = jnp.einsum("bij,kbi->kbj", tiles, picked_two, precision=highest)
    onehot_two = (cols_here[:, None] == jnp.arange(col_blocks)[None, :]).astype(jnp.float32)
    part_two = jnp.einsum("kbj,bq->kqj", terms_two, onehot_two, precision=highest).reshape(
        count, col_blocks * BLK
    )
    own_diag = diag_energy[None, :] * vectors
    metric_local = jnp.dot(
        vectors, vectors.T, precision=highest, preferred_element_type=jnp.float32
    )
    first = lax.psum_scatter(part_one, "col", scatter_dimension=1, tiled=True)
    second = lax.psum_scatter(part_two, "row", scatter_dimension=1, tiled=True)
    image = first + second + own_diag
    quad = jnp.dot(row_whole, part_one.T, precision=highest, preferred_element_type=jnp.float32)
    gram_local = (
        quad
        + quad.T
        + jnp.dot(vectors, own_diag.T, precision=highest, preferred_element_type=jnp.float32)
    )
    gram, metric = lax.psum((gram_local, metric_local), ("row", "col"))
    coef = solve_metric(metric, gram)
    resid = image - jnp.dot(coef.T, vectors, precision=highest, preferred_element_type=jnp.float32)
    return (image, resid)


def solution(mesh):
    return jax.shard_map(
        per_device,
        mesh=mesh,
        in_specs=(
            P(None, ("row", "col")),
            P(("row", "col")),
            P("row", "col", None, None),
            P("row", "col"),
            P("row", "col"),
        ),
        out_specs=(P(None, ("row", "col")), P(None, ("row", "col"))),
        check_vma=False,
    )
```

profile of v0, /device:TPU:0, one launch (start us, length us, event | category | flops | bytes accessed | tf_op | source)
XLA Modules:
  0.0 156.3 jit_solution(4022144908604003280)
XLA Ops:
  7.2 32.7 %all_gather.7 = f32[16,1024]{1,0:T(8,128)S(1)} all-gather(f32[16,128]{1,0:T(8,128)} %param.5), channel_id=1, replica_groups=mesh['row'=4,'col'=8] {'col'}, dimensions={1}, use_global_device_ids=true | all-gather | bytes 73728 | tf_op jit(solution)/shard_map/all_gather | solution.py:44
  39.9 0.7 fusion.288
  41.2 1.4 fusion.7
  42.9 0.6 copy.32
  43.6 5.2 %all_gather.6 = f32[16,512]{1,0:T(8,128)S(1)} all-gather(f32[16,128]{1,0:T(8,128)S(1)} %copy-done.1), channel_id=1, replica_groups=mesh['row'=4,'col'=8] {'row'}, dimensions={1}, use_global_device_ids=true | all-gather | bytes 40960 | tf_op jit(solution)/shard_map/all_gather | solution.py:43
  49.4 2.5 %fusion.4 = f32[16,24,128]{2,0,1:T(8,128)S(1)} fusion(f32[1,24,128,128]{3,2,1,0:T(8,128)S(1)} %copy-done, f32[24,16,128]{2,1,0:T(8,128)S(1)} %gather_fusion), kind=kOutput, calls=%fused_computation.6 | convolution fusion | flops 75497472 | bytes 1966080 | tf_op jit(solution)/shard_map/bij,kbj->kbi/dot_general | solution.py:50
  52.2 0.6 copy.31
  53.5 39.6 %all-reduce = (f32[16,16]{1,0:T(8,128)S(1)}, f32[16,16]{1,0:T(8,128)S(1)}) all-reduce(f32[16,16]{1,0:T(8,128)S(1)} %fusion.10, f32[16,16]{1,0:T(8,128)S(1)} %fusion.342), channel_id=1, replica_groups=mesh['row'=4,'col'=8] {'row','col'}, use_global_device_ids=true, to_apply=%region_2.0 | all-reduce | flops 512 | bytes 4096 | tf_op jit(solution)/shard_map/psum | solution.py:74
  94.2 0.6 slice.402
  97.8 0.6 slice.408
  99.5 0.6 slice.411
  111.7 0.6 slice.432
  113.4 0.6 slice.435
  120.0 0.7 fusion.341
  121.2 0.7 fusion.59
  121.9 0.9 fusion.60
  122.8 0.9 fusion.61
  123.7 0.8 fusion.62
  124.4 0.8 fusion.63
  125.2 0.8 fusion.64
  126.1 0.8 fusion.65
  126.9 0.8 fusion.66
  127.8 0.8 fusion.67
  128.6 0.8 fusion.68
  129.4 0.8 fusion.69
  130.2 0.8 fusion.70
  131.2 0.8 fusion.71
  132.0 0.8 fusion.72
  132.7 0.9 fusion.73
  133.6 0.9 fusion.74
  134.5 0.8 fusion.75
  135.3 0.8 fusion.76
  136.2 0.8 fusion.77
  136.9 0.9 fusion.78
  137.8 0.8 fusion.79
  138.7 0.8 fusion.80
  139.5 0.8 fusion.81
  140.3 0.9 fusion.82
  141.3 0.7 fusion.83
  142.0 0.8 fusion.84
  142.8 0.8 fusion.85
  143.6 0.8 fusion.86
  144.6 0.7 fusion.87
  145.2 0.9 fusion.88
  146.1 0.9 fusion.89
  147.0 0.8 fusion.90
  147.8 0.7 multiply_add_fusion.2
  148.5 0.9 convolution_subtract_fusion
  (119 shorter events, 16.5 us)
Async XLA Ops:
  7.2 34.0 %copy-start = (f32[1,24,128,128]{3,2,1,0:T(8,128)S(1)}, f32[1,24,128,128]{3,2,1,0:T(8,128)}, u32[]{:S(2)}) copy-start(f32[1,24,128,128]{3,2,1,0:T(8,128)} %param.7) | copy-start | bytes 4718596
  7.2 36.4 %copy-start.1 = (f32[16,128]{1,0:T(8,128)S(1)}, f32[16,128]{1,0:T(8,128)}, u32[]{:S(2)}) copy-start(f32[16,128]{1,0:T(8,128)} %param.5) | copy-start | bytes 24580
  7.2 35.5 %copy-start.4 = (s32[1,24]{1,0:T(1,128)S(1)}, s32[1,24]{1,0:T(1,128)}, u32[]{:S(2)}) copy-start(s32[1,24]{1,0:T(1,128)} %param.9) | copy-start | bytes 292
  7.2 140.6 %reduce-scatter.5.cloned.1.call-start = ((), (), s32[]{:S(2)}) async-start(), calls=%async_computation.3 | async-start | bytes 40960 | tf_op jit(solution)/shard_map/reduce_scatter | solution.py:66
  42.6 9.3 %copy-start.5 = (s32[1,24]{1,0:T(1,128)S(1)}, s32[1,24]{1,0:T(1,128)}, u32[]{:S(2)}) copy-start(s32[1,24]{1,0:T(1,128)} %param.8) | copy-start | bytes 292
  43.5 9.8 %copy-start.3 = (f32[128]{0:T(128)S(1)}, f32[128]{0:T(128)}, u32[]{:S(2)}) copy-start(f32[128]{0:T(128)} %param.6) | copy-start | bytes 1540
  43.5 104.3 %reduce-scatter.3.cloned.1.call-start = ((), (), s32[]{:S(2)}) async-start(), calls=%async_computation.2 | async-start | bytes 73728 | tf_op jit(solution)/shard_map/reduce_scatter | solution.py:65
  148.5 0.9 copy-start.2
Sparse Core Ops, SparseCore 0:
  43.6 20.4 reduce-scatter.4
  67.2 55.0 reduce-scatter.2
where the time goes:
time: 157 us; the launch traced here: 156 us
  blocking collectives  77.5 us (49%)
  matrix products  34.4 us (22%)
  between operations  25 us (16%)
  local copies, waits for them, and re-layouts  15.8 us (10%)
  other arithmetic  3.43 us (2%)
    psum x1, blocking collectives, per_device(): gram, metric = lax.psum((gram_local, metric_local), ('row', 'col'))  39.6 us
    all_gather x1, blocking collectives, per_device(): row_whole = lax.all_gather(vectors, 'col', axis=1, tiled=True)  32.7 us
    dot_general x16, matrix products, solve_metric(): jnp.dot(factor[:, line], solved, precision=highest)  13 us
    dot_general x16, matrix products, solve_metric(): jnp.dot(factor[line, :], inner, precision=highest)  13 us
    slice x15, local copies, waits for them, and re-layouts, solve_metric(): pivot = jnp.sqrt(rest[column])  8.98 us
    all_gather x1, blocking collectives, per_device(): col_whole = lax.all_gather(vectors, 'row', axis=1, tiled=True)  5.19 us
  transfers between devices with their start and end apart: 2, of which 0 were waited for; matrix products, arithmetic and copies ran while one was open for 31% of the time, Pallas kernels for 0%

commit v1 on v0

--- a/solution.py
+++ b/solution.py
@@ -71,7 +71,7 @@
         + quad.T
         + jnp.dot(vectors, own_diag.T, precision=highest, preferred_element_type=jnp.float32)
     )
-    gram, metric = lax.psum((gram_local, metric_local), ("row", "col"))
+    gram, metric = lax.psum(lax.psum((gram_local, metric_local), "col"), "row")
     coef = solve_metric(metric, gram)
     resid = image - jnp.dot(coef.T, vectors, precision=highest, preferred_element_type=jnp.float32)
     return (image, resid)

time: 157 us -> 165 us (1.051)
  blocking collectives: 77.5 us -> 85.7 us
    psum x1 -> x2, blocking collectives: 39.6 us -> 47.8 us  [per_device(): gram, metric = lax.psum(lax.psum((gram_local, metric_local), 'col'), 'row')]
  transfers between devices with their start and end apart: 2 -> 2, of which waited for: 0 -> 0; matrix products, arithmetic and copies ran while one was open for 31% -> 30% of each run, Pallas kernels for 0% -> 0%
where the time goes in v1:
time: 165 us; the launch traced here: 164 us
  blocking collectives  85.7 us (52%)
  matrix products  34.4 us (21%)
  between operations  25 us (15%)
  local copies, waits for them, and re-layouts  15.8 us (10%)
  other arithmetic  3.43 us (2%)
    psum x2, blocking collectives, per_device(): gram, metric = lax.psum(lax.psum((gram_local, metric_local), 'col'), 'row')  47.8 us
    all_gather x1, blocking collectives, per_device(): row_whole = lax.all_gather(vectors, 'col', axis=1, tiled=True)  32.7 us
    dot_general x16, matrix products, solve_metric(): jnp.dot(factor[:, line], solved, precision=highest)  13 us
    dot_general x16, matrix products, solve_metric(): jnp.dot(factor[line, :], inner, precision=highest)  13 us
    slice x15, local copies, waits for them, and re-layouts, solve_metric(): pivot = jnp.sqrt(rest[column])  8.98 us
    all_gather x1, blocking collectives, per_device(): col_whole = lax.all_gather(vectors, 'row', axis=1, tiled=True)  5.19 us
  transfers between devices with their start and end apart: 2, of which 0 were waited for; matrix products, arithmetic and copies ran while one was open for 30% of the time, Pallas kernels for 0%

profile of v1, /device:TPU:0, one launch (start us, length us, event | category | flops | bytes accessed | tf_op | source)
XLA Modules:
  0.0 164.4 jit_solution(5783769482973737964)
XLA Ops:
  7.2 32.7 %all_gather.7 = f32[16,1024]{1,0:T(8,128)S(1)} all-gather(f32[16,128]{1,0:T(8,128)} %param.5), channel_id=1, replica_groups=mesh['row'=4,'col'=8] {'col'}, dimensions={1}, use_global_device_ids=true | all-gather | bytes 73728 | tf_op jit(solution)/shard_map/all_gather | solution.py:44
  39.9 0.7 fusion.288
  41.2 1.4 fusion.7
  42.9 0.6 copy.32
  43.6 5.2 %all_gather.6 = f32[16,512]{1,0:T(8,128)S(1)} all-gather(f32[16,128]{1,0:T(8,128)S(1)} %copy-done.1), channel_id=1, replica_groups=mesh['row'=4,'col'=8] {'row'}, dimensions={1}, use_global_device_ids=true | all-gather | bytes 40960 | tf_op jit(solution)/shard_map/all_gather | solution.py:43
  49.4 2.5 %fusion.4 = f32[16,24,128]{2,0,1:T(8,128)S(1)} fusion(f32[1,24,128,128]{3,2,1,0:T(8,128)S(1)} %copy-done, f32[24,16,128]{2,1,0:T(8,128)S(1)} %gather_fusion), kind=kOutput, calls=%fused_computation.6 | convolution fusion | flops 75497472 | bytes 1966080 | tf_op jit(solution)/shard_map/bij,kbj->kbi/dot_general | solution.py:50
  52.2 0.6 copy.31
  53.5 37.0 %all-reduce = (f32[16,16]{1,0:T(8,128)S(1)}, f32[16,16]{1,0:T(8,128)S(1)}) all-reduce(f32[16,16]{1,0:T(8,128)S(1)} %fusion.10, f32[16,16]{1,0:T(8,128)S(1)} %fusion.342), channel_id=1, replica_groups=mesh['row'=4,'col'=8] {'col'}, use_global_device_ids=true, to_apply=%region_2.0 | all-reduce | flops 512 | bytes 4096 | tf_op jit(solution)/shard_map/psum | solution.py:74
  90.5 10.8 %all-reduce.1 = (f32[16,16]{1,0:T(8,128)S(1)}, f32[16,16]{1,0:T(8,128)S(1)}) all-reduce(f32[16,16]{1,0:T(8,128)S(1)} %get-tuple-element.34, f32[16,16]{1,0:T(8,128)S(1)} %get-tuple-element.35), channel_id=1, replica_groups=mesh['row'=4,'col'=8] {'row'}, use_global_device_ids=true, to_apply=%region_3.0 | all-reduce | flops 512 | bytes 4096 | tf_op jit(solution)/shard_map/psum | solution.py:74
  102.4 0.6 slice.402
  105.9 0.6 slice.408
  107.7 0.6 slice.411
  111.3 0.6 slice.417
  128.2 0.7 fusion.341
  129.3 0.7 fusion.59
  130.0 0.9 fusion.60
  130.9 0.9 fusion.61
  131.8 0.8 fusion.62
  132.6 0.8 fusion.63
  133.4 0.8 fusion.64
  134.2 0.8 fusion.65
  135.1 0.8 fusion.66
  136.0 0.8 fusion.67
  136.7 0.8 fusion.68
  137.5 0.8 fusion.69
  138.4 0.8 fusion.70
  139.3 0.8 fusion.71
  140.1 0.8 fusion.72
  140.9 0.9 fusion.73
  141.7 0.9 fusion.74
  142.7 0.8 fusion.75
  143.5 0.8 fusion.76
  144.3 0.8 fusion.77
  145.1 0.9 fusion.78
  146.0 0.8 fusion.79
  146.8 0.8 fusion.80
  147.7 0.8 fusion.81
  148.5 0.9 fusion.82
  149.4 0.7 fusion.83
  150.1 0.8 fusion.84
  151.0 0.8 fusion.85
  151.8 0.8 fusion.86
  152.7 0.7 fusion.87
  153.4 0.9 fusion.88
  154.3 0.9 fusion.89
  155.2 0.8 fusion.90
  156.0 0.7 multiply_add_fusion.2
  156.7 0.9 convolution_subtract_fusion
  (120 shorter events, 17.1 us)
Async XLA Ops:
  7.2 34.0 %copy-start = (f32[1,24,128,128]{3,2,1,0:T(8,128)S(1)}, f32[1,24,128,128]{3,2,1,0:T(8,128)}, u32[]{:S(2)}) copy-start(f32[1,24,128,128]{3,2,1,0:T(8,128)} %param.7) | copy-start | bytes 4718596
  7.2 36.4 %copy-start.1 = (f32[16,128]{1,0:T(8,128)S(1)}, f32[16,128]{1,0:T(8,128)}, u32[]{:S(2)}) copy-start(f32[16,128]{1,0:T(8,128)} %param.5) | copy-start | bytes 24580
  7.2 35.5 %copy-start.4 = (s32[1,24]{1,0:T(1,128)S(1)}, s32[1,24]{1,0:T(1,128)}, u32[]{:S(2)}) copy-start(s32[1,24]{1,0:T(1,128)} %param.9) | copy-start | bytes 292
  7.2 148.8 %reduce-scatter.5.cloned.1.call-start = ((), (), s32[]{:S(2)}) async-start(), calls=%async_computation.3 | async-start | bytes 40960 | tf_op jit(solution)/shard_map/reduce_scatter | solution.py:66
  42.6 9.3 %copy-start.5 = (s32[1,24]{1,0:T(1,128)S(1)}, s32[1,24]{1,0:T(1,128)}, u32[]{:S(2)}) copy-start(s32[1,24]{1,0:T(1,128)} %param.8) | copy-start | bytes 292
  43.5 9.8 %copy-start.3 = (f32[128]{0:T(128)S(1)}, f32[128]{0:T(128)}, u32[]{:S(2)}) copy-start(f32[128]{0:T(128)} %param.6) | copy-start | bytes 1540
  43.5 112.4 %reduce-scatter.3.cloned.1.call-start = ((), (), s32[]{:S(2)}) async-start(), calls=%async_computation.2 | async-start | bytes 73728 | tf_op jit(solution)/shard_map/reduce_scatter | solution.py:65
  156.7 0.9 copy-start.2
Sparse Core Ops, SparseCore 0:
  43.6 20.4 reduce-scatter.4
  67.2 55.0 reduce-scatter.2
